TPU v7x, 32 devices: a whole 2x2x4 slice. The times are simulated.
32 devices in a mesh: freq: 4 (over y, x), panel: 8 (over z, core).
Axes of the slice: x: 2, y: 2, z: 4, core: 2. Of those that a mesh axis runs over, the one named last changes fastest.
Arguments:
- traces: bfloat16 [640, 640, 1024], P('panel', 'freq'), may hold values from -6 to 6
- filters: float32 [16, 7, 64], replicated, may hold values from -0.25 to 0.25
Outputs:
- primaries: bfloat16 [640, 640, 1024], P('panel', 'freq')
All inputs are finite; a program needn't handle non-finite values.
Results may differ from a plain program's by a relative error of at most 0.0095.
Values may be sent and summed in bfloat16 or wider, within the bound.
A program may use at most 192 MiB of HBM per device.

v0:
```python
import math
import jax
import jax.numpy as jnp
from jax import lax
from jax.sharding import PartitionSpec as P

NS = 640
NT = 1024
NF = 96
FLO = 8
TAPS = 64
SPAN = 7
RWIN = 40


def wave_table(freq_bins, sample_index):
    phases = freq_bins[:, None] * sample_index[None, :] % NT
    angles = phases.astype(jnp.float32) * jnp.float32(2.0 * math.pi / NT)
    return (jnp.cos(angles), jnp.sin(angles))


def complex_product(left_side, right_side):

    def factor_product(leading_factor, trailing_factor):
        return jnp.einsum(
            "gjo,god->gjd", leading_factor, trailing_factor, preferred_element_type=jnp.float32
        )

    part_real = factor_product(left_side[0], right_side[0]) - factor_product(
        left_side[1], right_side[1]
    )
    part_imag = factor_product(left_side[0], right_side[1]) + factor_product(
        left_side[1], right_side[0]
    )
    return jnp.stack([part_real, part_imag])


def response(filters, freq_bins):
    tap_index = jnp.arange(TAPS, dtype=jnp.int32)
    cosine_wave, sine_wave = wave_table(freq_bins, tap_index)
    filter_real = jnp.einsum("fk,wjk->fjw", cosine_wave, filters, precision=lax.Precision.HIGHEST)
    filter_imag = -jnp.einsum("fk,wjk->fjw", sine_wave, filters, precision=lax.Precision.HIGHEST)
    return (jnp.repeat(filter_real, RWIN, axis=2), jnp.repeat(filter_imag, RWIN, axis=2))


def apply_filter(extended, filter_real, filter_imag, source_count):
    sum_real = jnp.zeros(extended.shape[1:2] + (source_count,) + extended.shape[3:], jnp.float32)
    sum_imag = jnp.zeros_like(sum_real)
    for shifted in range(SPAN):
        part_real = extended[0, :, shifted : shifted + source_count, :]
        part_imag = extended[1, :, shifted : shifted + source_count, :]
        weight_real = filter_real[:, shifted][:, None, :]
        weight_imaginary = filter_imag[:, shifted][:, None, :]
        sum_real = sum_real + weight_real * part_real - weight_imaginary * part_imag
        sum_imag = sum_imag + weight_real * part_imag + weight_imaginary * part_real
    return jnp.stack([sum_real, sum_imag])


def per_device(traces, filters):
    shot_rows, receiver_cols, time_sample_count = traces.shape
    rim_width = SPAN // 2
    scale_sources = jnp.float32(math.sqrt(NS))
    freq_bins = FLO + jnp.arange(NF, dtype=jnp.int32)
    cosine_wave, sine_wave = wave_table(freq_bins, jnp.arange(NT, dtype=jnp.int32))
    forward = (jnp.concatenate([cosine_wave, -sine_wave], 0) / jnp.float32(math.sqrt(NT))).astype(
        jnp.bfloat16
    )
    reciprocal_value = jnp.concatenate([cosine_wave, -sine_wave], 0).astype(jnp.bfloat16)
    spectra = jnp.einsum("srt,ct->csr", traces, forward, preferred_element_type=jnp.float32)
    spectra = spectra.astype(jnp.bfloat16).reshape(2, NF, shot_rows, receiver_cols)
    columns = lax.all_to_all(spectra, "panel", split_axis=1, concat_axis=2, tiled=True)
    slice_count = columns.shape[1]
    first_slice = lax.axis_index("panel") * slice_count
    complete = lax.all_gather(columns, "freq", axis=3, tiled=True)
    order_one = (complex_product(complete, columns) / scale_sources).astype(jnp.bfloat16)
    order_two = complex_product(complete, order_one) / scale_sources
    prediction = (order_one.astype(jnp.float32) - order_two).astype(jnp.bfloat16)
    extended = jnp.pad(
        prediction.astype(jnp.float32), ((0, 0), (0, 0), (rim_width, rim_width), (0, 0))
    )
    own_bins = FLO + first_slice + jnp.arange(slice_count, dtype=jnp.int32)
    filter_real, filter_imag = response(filters, own_bins)
    receiver_start = lax.axis_index("freq") * receiver_cols
    filter_real = lax.dynamic_slice_in_dim(filter_real, receiver_start, receiver_cols, 2)
    filter_imag = lax.dynamic_slice_in_dim(filter_imag, receiver_start, receiver_cols, 2)
    matched = apply_filter(extended, filter_real, filter_imag, NS)
    returned = lax.all_to_all(
        matched.astype(jnp.bfloat16), "panel", split_axis=2, concat_axis=1, tiled=True
    )
    matched_rows = returned.reshape(2 * NF, shot_rows, receiver_cols)
    multiples = jnp.einsum(
        "csr,ct->srt", matched_rows, reciprocal_value, preferred_element_type=jnp.float32
    )
    multiples = multiples / jnp.float32(math.sqrt(NF))
    return (traces.astype(jnp.float32) - multiples).astype(jnp.bfloat16)


def solution(mesh):
    placed = (P("panel", "freq", None), P())
    return jax.shard_map(
        per_device, mesh=mesh, in_specs=placed, out_specs=P("panel", "freq", None), check_vma=False
    )
```

profile of v0, /device:TPU:0, one launch (start us, length us, event | category | flops | bytes accessed | tf_op | source)
XLA Modules:
  0.0 942.0 jit_solution(9572457835950158956)
XLA Ops:
  6.5 0.0 copy-start
  6.5 0.0 all-gather.2.cloned.1.call-start
  6.5 1.6 fusion.42
  8.2 0.0 copy-start.3
  8.2 0.7 copy-done.3
  8.9 0.2 copy-done.5
  9.1 13.8 %convolution_convert_fusion = bf16[192,80,160]{0,2,1:T(8,128)(2,1)} fusion(bf16[80,160,1024]{2,1,0:T(8,128)(2,1)} %param.2, f32[96,1024]{1,0:T(8,128)S(1)} %get-tuple-element.24, f32[96,1024]{1,0:T(8,128)S(1)} %get-tuple-element.23), kind=kOutput, calls=%fused_computation.35 | convolution fusion | flops 5036212224 | bytes 31916032 | tf_op jit(solution)/shard_map/srt,ct->csr/dot_general | solution.py:69
  22.9 15.0 %reshape.26 = bf16[2,96,80,160]{1,0,3,2:T(2,128)(2,1)} reshape(bf16[192,80,160]{0,2,1:T(8,128)(2,1)} %convolution_convert_fusion) | data formatting | bytes 9830400 | tf_op jit(solution)/shard_map/reshape | solution.py:70
  37.9 17.3 %copy.39 = bf16[2,96,80,160]{3,2,0,1:T(8,128)(2,1)} copy(bf16[2,96,80,160]{1,0,3,2:T(2,128)(2,1)} %reshape.26) | data formatting | bytes 9830400 | tf_op jit(solution)/shard_map/reshape | solution.py:70
  55.2 179.6 %all_to_all.33 = bf16[2,96,80,160]{3,2,0,1:T(8,128)(2,1)} all-to-all(bf16[2,96,80,160]{3,2,0,1:T(8,128)(2,1)} %copy.39), channel_id=1, replica_groups=mesh['freq'=4,'panel'=8] {'panel'}, dimensions={1} | all-to-all | bytes 9830400 | tf_op jit(solution)/shard_map/all_to_all | solution.py:71
  234.8 12.6 %copy.52 = bf16[2,12,8,80,160]{3,2,0,1,4:T(8,128)(2,1)} copy(bf16[2,12,8,80,160]{4,3,0,1,2:T(8,128)(2,1)} %bitcast.133) | data formatting | bytes 9830400 | tf_op jit(solution)/shard_map/all_to_all | solution.py:71
  247.4 16.3 %reshape.33 = bf16[2,12,640,160]{2,0,1,3:T(2,128)(2,1)} reshape(bf16[2,12,8,80,160]{3,2,0,1,4:T(8,128)(2,1)} %copy.52) | data formatting | bytes 9830400 | tf_op jit(solution)/shard_map/all_to_all | solution.py:71
  263.7 0.0 all-gather.2.cloned.1.call-update
  263.8 0.6 fusion.29
  264.4 0.6 convolution_bitcast_fusion
  265.0 0.2 broadcast_in_dim.4
  265.2 0.4 reshape.25
  265.6 0.2 broadcast_in_dim.5
  265.9 0.4 reshape.27
  266.3 0.5 constant_dynamic-slice_fusion.10
  266.9 0.6 copy.99
  267.5 4.5 copy.40
  272.0 4.5 fusion.67
  276.5 6.7 copy.46
  283.2 5.5 squeeze.15
  288.7 6.4 copy.44
  295.1 6.6 squeeze.13
  301.7 144.0 %all-gather.2.cloned.1.call-done = bf16[2,12,640,640]{2,0,1,3:T(2,128)(2,1)} async-done(((bf16[2,12,640,160]{2,0,1,3:T(2,128)(2,1)}), bf16[2,12,640,640]{2,0,1,3:T(2,128)(2,1)}) %all-gather.2.cloned.1.call-update) | async-done | bytes 19660816 | tf_op jit(solution)/shard_map/all_gather | solution.py:74
  445.7 38.6 %fusion.66 = (bf16[1,12,640,640]{2,0,1,3:T(2,128)(2,1)}, bf16[1,12,640,640]{2,0,1,3:T(2,128)(2,1)}) fusion(bf16[2,12,640,640]{2,0,1,3:T(2,128)(2,1)} %all-gather.2.cloned.1.call-done), kind=kLoop, calls=%fused_computation.120 | loop fusion | bytes 39321600 | tf_op jit(solution)/shard_map/slice | solution.py:29
  484.4 38.2 %copy.68 = bf16[1,12,640,640]{3,2,1,0:T(8,128)(2,1)} copy(bf16[1,12,640,640]{2,0,1,3:T(2,128)(2,1)} %get-tuple-element.5) | data formatting | bytes 19660800
  522.6 38.4 %copy.69 = bf16[1,12,640,640]{3,2,1,0:T(8,128)(2,1)} copy(bf16[1,12,640,640]{2,0,1,3:T(2,128)(2,1)} %get-tuple-element.6) | data formatting | bytes 19660800
  561.0 10.0 %fusion.7 = f32[12,640,160]{1,2,0:T(8,128)} fusion(bf16[12,640,160]{1,2,0:T(8,128)(2,1)} %squeeze.13, bf16[1,12,640,640]{3,2,1,0:T(8,128)(2,1)} %copy.69), kind=kOutput, calls=%fused_computation.22 | convolution fusion | flops 1572864000 | bytes 17203200 | tf_op jit(solution)/shard_map/gjo,god->gjd/dot_general | solution.py:25
  571.0 9.3 fusion.9
  580.3 10.8 %add_bitcast_fusion.1 = f32[1,12,640,160]{2,3,1,0:T(8,128)} fusion(f32[12,640,160]{1,2,0:T(8,128)} %fusion.7, bf16[12,640,160]{1,2,0:T(8,128)(2,1)S(1)} %squeeze.15, bf16[1,12,640,640]{3,2,1,0:T(8,128)(2,1)} %copy.68), kind=kOutput, calls=%fused_computation.42 | convolution fusion | flops 1574092800 | bytes 22118400 | tf_op jit(solution)/shard_map/gjo,god->gjd/dot_general | solution.py:25
  591.1 11.4 %subtract_bitcast_fusion.1 = f32[1,12,640,160]{2,3,1,0:T(8,128)} fusion(f32[12,640,160]{1,2,0:T(8,128)} %fusion.9, bf16[12,640,160]{1,2,0:T(8,128)(2,1)} %squeeze.13, bf16[1,12,640,640]{3,2,1,0:T(8,128)(2,1)} %copy.68), kind=kOutput, calls=%fused_computation.43 | convolution fusion | flops 1574092800 | bytes 22118400 | tf_op jit(solution)/shard_map/gjo,god->gjd/dot_general | solution.py:25
  602.6 5.1 fusion
  607.6 11.4 %fusion.3 = f32[12,640,160]{1,2,0:T(8,128)} fusion(bf16[1,12,640,640]{3,2,1,0:T(8,128)(2,1)} %copy.69, bf16[2,12,640,160]{2,3,1,0:T(8,128)(2,1)S(1)} %fusion), kind=kOutput, calls=%fused_computation.18 | convolution fusion | flops 1572864000 | bytes 17203200 | tf_op jit(solution)/shard_map/gjo,god->gjd/dot_general | solution.py:25
  619.0 9.3 fusion.5
  628.4 11.5 %subtract_bitcast_fusion = f32[1,12,640,160]{2,3,1,0:T(8,128)} fusion(f32[12,640,160]{1,2,0:T(8,128)} %fusion.5, bf16[1,12,640,640]{3,2,1,0:T(8,128)(2,1)} %copy.68, bf16[2,12,640,160]{2,3,1,0:T(8,128)(2,1)} %copy-done.2), kind=kOutput, calls=%fused_computation.41 | convolution fusion | flops 1574092800 | bytes 22118400 | tf_op jit(solution)/shard_map/gjo,god->gjd/dot_general | solution.py:25
  639.8 11.5 %add_bitcast_fusion = f32[1,12,640,160]{2,3,1,0:T(8,128)} fusion(f32[12,640,160]{1,2,0:T(8,128)} %fusion.3, bf16[1,12,640,640]{3,2,1,0:T(8,128)(2,1)} %copy.68, bf16[2,12,640,160]{2,3,1,0:T(8,128)(2,1)} %copy-done.2), kind=kOutput, calls=%fused_computation.40 | convolution fusion | flops 1574092800 | bytes 22118400 | tf_op jit(solution)/shard_map/gjo,god->gjd/dot_general | solution.py:25
  651.3 7.4 fusion.20
  658.8 21.9 %add_convert_fusion = bf16[1,12,640,160]{2,3,1,0:T(8,128)(2,1)S(1)} fusion(f32[2,12,640,160]{2,3,1,0:T(8,128)S(1)} %fusion.20, f32[12,160]{1,0:T(8,128)S(1)} %bitcast.149, f32[12,160]{1,0:T(8,128)S(1)} %bitcast.151, f32[12,160]{1,0:T(8,128)S(1)} %bitcast.139, f32[12,160]{1,0:T(8,128)S(1)} %bitcast.161, f32[12,160]{1,0:T(8,128)S(1)} %bitcast.141, ...), kind=kLoop, calls=%fused_computation.38 | loop fusion | flops 34406400 | bytes 22347776 | tf_op jit(solution)/shard_map/convert.1
  680.6 21.9 %subtract_convert_fusion.1 = bf16[1,12,640,160]{2,3,1,0:T(8,128)(2,1)S(1)} fusion(f32[2,12,640,160]{2,3,1,0:T(8,128)S(1)} %fusion.20, f32[12,160]{1,0:T(8,128)S(1)} %bitcast.150, f32[12,160]{1,0:T(8,128)S(1)} %bitcast.152, f32[12,160]{1,0:T(8,128)S(1)} %bitcast.140, f32[12,160]{1,0:T(8,128)S(1)} %bitcast.162, f32[12,160]{1,0:T(8,128)S(1)} %bitcast.142, ...), kind=kLoop, calls=%fused_computation.39 | loop fusion | flops 34406400 | bytes 22347776 | tf_op jit(solution)/shard_map/convert
  702.6 2.7 pad_maximum_fusion
  705.3 19.4 %copy.48 = bf16[2,12,640,160]{3,0,1,2:T(2,128)(2,1)} copy(bf16[2,12,640,160]{2,3,1,0:T(8,128)(2,1)} %pad_maximum_fusion) | data formatting | bytes 9830400 | tf_op jit(solution)/shard_map/stack | solution.py:56
  724.7 177.2 %all_to_all.34 = bf16[2,12,640,160]{3,0,1,2:T(2,128)(2,1)S(1)} all-to-all(bf16[2,12,640,160]{3,0,1,2:T(2,128)(2,1)} %copy.48), channel_id=1, replica_groups=mesh['freq'=4,'panel'=8] {'panel'}, dimensions={2} | all-to-all | bytes 9830400 | tf_op jit(solution)/shard_map/all_to_all | solution.py:87
  902.0 4.9 copy.49
  906.9 27.9 %subtract_convert_fusion = bf16[80,160,1024]{2,1,0:T(8,128)(2,1)} fusion(bf16[80,160,1024]{2,1,0:T(8,128)(2,1)} %param.2, bf16[192,80,160]{2,1,0:T(8,128)(2,1)} %bitcast.136, f32[96,1024]{1,0:T(8,128)S(1)} %copy-done.6, f32[96,1024]{1,0:T(8,128)S(1)} %copy-done.4), kind=kOutput, calls=%fused_computation | convolution fusion | flops 5086380032 | bytes 58130432 | tf_op jit(solution)/shard_map/csr,ct->srt/dot_general | solution.py:91
  (29 shorter events, 0.1 us)
Async XLA Ops:
  6.5 257.3 %copy-start = (f32[16,7,64]{2,0,1:T(8,128)S(1)}, f32[16,7,64]{2,0,1:T(8,128)}, u32[]{:S(2)}) copy-start(f32[16,7,64]{2,0,1:T(8,128)} %param.3) | copy-start | bytes 86020
  6.5 439.2 %all-gather.2.cloned.1.call-start = ((), (), s32[]{:S(2)}) async-start(), calls=%async_computation.2 | async-start | bytes 24576000 | tf_op jit(solution)/shard_map/all_gather | solution.py:74
  8.2 0.7 copy-start.3
  8.2 0.9 copy-start.5
  607.6 11.4 %copy-start.2 = (bf16[2,12,640,160]{2,3,1,0:T(8,128)(2,1)}, bf16[2,12,640,160]{2,3,1,0:T(8,128)(2,1)S(1)}, u32[]{:S(2)}) copy-start(bf16[2,12,640,160]{2,3,1,0:T(8,128)(2,1)S(1)} %fusion) | copy-start | bytes 14745604
  651.3 7.4 copy-start.7
  901.9 4.9 copy-start.4
  902.0 4.9 copy-start.6
  906.9 27.9 %copy-start.1 = (f32[16,7,64]{2,0,1:T(8,128)S(1)}, f32[16,7,64]{2,0,1:T(8,128)}, u32[]{:S(2)}) copy-start(f32[16,7,64]{2,0,1:T(8,128)} %param.3) | copy-start | bytes 86020
Sparse Core Ops, SparseCore 0:
  263.9 181.7 all-gather.1
where the time goes:
time: 952 us; the launch traced here: 942 us
  blocking collectives  357 us (38%)
  local copies, waits for them, and re-layouts  238 us (25%)
  waiting for transfers between devices  144 us (15%)
  matrix products  128 us (13%)
  other arithmetic  60.6 us (6%)
  between operations  14.1 us (1%)
    all_to_all x1, blocking collectives, per_device(): lax.all_to_all(spectra, 'panel', split_axis=1, concat_axis=2, tiled=True)  180 us
    all_to_all x1, blocking collectives, per_device(): lax.all_to_all(matched.astype(jnp.bfloat16), 'panel', split_axis=2, conca...  177 us
    all_gather x1, waiting for transfers between devices, per_device(): complete = lax.all_gather(columns, 'freq', axis=3, tiled=True)  144 us
    dot_general x8, matrix products, factor_product(): jnp.einsum('gjo,god->gjd', leading_factor, trailing_factor, preferred_ele...  85.3 us
    unnamed x32, local copies, waits for them, and re-layouts  78.2 us
    another operation x2, other arithmetic  43.8 us
    slice x1, local copies, waits for them, and re-layouts, complex_product(): left_side[0]  38.6 us
    all_to_all x3, local copies, waits for them, and re-layouts, per_device(): lax.all_to_all(spectra, 'panel', split_axis=1, concat_axis=2, tiled=True)  33.4 us
  transfers between devices with their start and end apart: 1, of which 1 were waited for; matrix products, arithmetic and copies ran while one was open for 4% of the time, Pallas kernels for 0%

commit v1 on v0

--- a/solution.py
+++ b/solution.py
@@ -71,7 +71,8 @@
     columns = lax.all_to_all(spectra, "panel", split_axis=1, concat_axis=2, tiled=True)
     slice_count = columns.shape[1]
     first_slice = lax.axis_index("panel") * slice_count
-    complete = lax.all_gather(columns, "freq", axis=3, tiled=True)
+    terms = lax.all_gather(columns, "freq", axis=0, tiled=False)
+    complete = jnp.concatenate(terms, axis=3)
     order_one = (complex_product(complete, columns) / scale_sources).astype(jnp.bfloat16)
     order_two = complex_product(complete, order_one) / scale_sources
     prediction = (order_one.astype(jnp.float32) - order_two).astype(jnp.bfloat16)

time: 952 us -> 817 us (0.86)
  local copies, waits for them, and re-layouts: 238 us -> 144 us
  matrix products: 128 us -> 87.9 us
    unnamed x32 -> x28, local copies, waits for them, and re-layouts: 78.2 us -> 2.31 us
    dot_general x8, matrix products: 85.3 us -> 45.1 us  [factor_product(): jnp.einsum('gjo,god->gjd', leading_factor, trailing_factor, preferred_ele...]
    slice x1, local copies, waits for them, and re-layouts: 38.6 us -> 8.21 us  [complex_product(): left_side[0]]
    all_gather x0 -> x2, local copies, waits for them, and re-layouts: none -> 29.2 us  [per_device(): terms = lax.all_gather(columns, 'freq', axis=0, tiled=False)]
    all_to_all x3 -> x2, local copies, waits for them, and re-layouts: 33.4 us -> 15.7 us  [per_device(): lax.all_to_all(spectra, 'panel', split_axis=1, concat_axis=2, tiled=True)]
  transfers between devices with their start and end apart: 1 -> 1, of which waited for: 1 -> 1; matrix products, arithmetic and copies ran while one was open for 4% -> 5% of each run, Pallas kernels for 0% -> 0%
where the time goes in v1:
time: 817 us; the launch traced here: 808 us
  blocking collectives  357 us (44%)
  local copies, waits for them, and re-layouts  144 us (18%)
  waiting for transfers between devices  144 us (18%)
  matrix products  87.9 us (11%)
  other arithmetic  60.4 us (7%)
  between operations  14.1 us (2%)
    all_to_all x1, blocking collectives, per_device(): lax.all_to_all(spectra, 'panel', split_axis=1, concat_axis=2, tiled=True)  180 us
    all_to_all x1, blocking collectives, per_device(): lax.all_to_all(matched.astype(jnp.bfloat16), 'panel', split_axis=2, conca...  178 us
    all_gather x1, waiting for transfers between devices, per_device(): terms = lax.all_gather(columns, 'freq', axis=0, tiled=False)  144 us
    dot_general x8, matrix products, factor_product(): jnp.einsum('gjo,god->gjd', leading_factor, trailing_factor, preferred_ele...  45.1 us
    another operation x2, other arithmetic  43.6 us
    reshape x2, local copies, waits for them, and re-layouts, per_device(): spectra.astype(jnp.bfloat16).reshape(2, NF, shot_rows, receiver_cols)  32.3 us
    all_gather x2, local copies, waits for them, and re-layouts, per_device(): terms = lax.all_gather(columns, 'freq', axis=0, tiled=False)  29.2 us
    dot_general x1, matrix products, per_device(): jnp.einsum('csr,ct->srt', matched_rows, reciprocal_value, preferred_eleme...  27.9 us
  transfers between devices with their start and end apart: 1, of which 1 were waited for; matrix products, arithmetic and copies ran while one was open for 5% of the time, Pallas kernels for 0%

profile of v1, /device:TPU:0, one launch (start us, length us, event | category | flops | bytes accessed | tf_op | source)
XLA Modules:
  0.0 808.3 jit_solution(12509804548485124335)
XLA Ops:
  6.5 0.0 copy-start
  6.5 0.0 all-gather.2.cloned.1.call-start
  6.5 1.6 fusion.22
  8.2 0.7 copy-done.3
  8.9 0.1 copy-done.5
  9.1 13.8 %convolution_convert_fusion = bf16[192,80,160]{0,2,1:T(8,128)(2,1)} fusion(bf16[80,160,1024]{2,1,0:T(8,128)(2,1)} %param.2, f32[96,1024]{1,0:T(8,128)S(1)} %get-tuple-element.24, f32[96,1024]{1,0:T(8,128)S(1)} %get-tuple-element.23), kind=kOutput, calls=%fused_computation.20 | convolution fusion | flops 5036212224 | bytes 31916032 | tf_op jit(solution)/shard_map/srt,ct->csr/dot_general | solution.py:69
  22.8 15.0 %reshape.35 = bf16[2,96,80,160]{1,0,3,2:T(2,128)(2,1)} reshape(bf16[192,80,160]{0,2,1:T(8,128)(2,1)} %convolution_convert_fusion) | data formatting | bytes 9830400 | tf_op jit(solution)/shard_map/reshape | solution.py:70
  37.8 17.3 %copy.59 = bf16[2,96,80,160]{3,2,0,1:T(8,128)(2,1)} copy(bf16[2,96,80,160]{1,0,3,2:T(2,128)(2,1)} %reshape.35) | data formatting | bytes 9830400 | tf_op jit(solution)/shard_map/reshape | solution.py:70
  55.2 179.6 %all_to_all.30 = bf16[2,96,80,160]{3,2,0,1:T(8,128)(2,1)} all-to-all(bf16[2,96,80,160]{3,2,0,1:T(8,128)(2,1)} %copy.59), channel_id=1, replica_groups=mesh['freq'=4,'panel'=8] {'panel'}, dimensions={1} | all-to-all | bytes 9830400 | tf_op jit(solution)/shard_map/all_to_all | solution.py:71
  234.8 11.6 %copy.61 = bf16[2,12,8,80,160]{3,2,4,1,0:T(8,128)(2,1)} copy(bf16[2,12,8,80,160]{4,3,0,1,2:T(8,128)(2,1)} %bitcast.133) | data formatting | bytes 9830400 | tf_op jit(solution)/shard_map/all_to_all | solution.py:71
  246.5 12.1 %all_gather.6 = bf16[1,2,12,640,160]{3,4,2,1,0:T(8,128)(2,1)} reshape(bf16[2,12,8,80,160]{3,2,4,1,0:T(8,128)(2,1)} %copy.61) | data formatting | bytes 9830400 | tf_op jit(solution)/shard_map/all_gather | solution.py:74
  258.6 0.0 all-gather.2.cloned.1.call-update
  258.6 0.6 convolution_bitcast_fusion
  259.2 0.2 broadcast_in_dim.4
  259.5 0.4 reshape.34
  259.9 0.6 fusion.9
  260.5 0.2 broadcast_in_dim.5
  260.7 0.4 reshape.37
  261.1 0.5 constant_dynamic-slice_fusion.10
  261.8 4.0 copy.60
  265.8 4.8 fusion.47
  270.6 6.9 copy.63
  277.6 5.5 squeeze.13
  283.1 6.4 copy.65
  289.5 6.6 squeeze.15
  296.1 144.4 %all-gather.2.cloned.1.call-done = bf16[4,2,12,640,160]{3,4,2,1,0:T(8,128)(2,1)} async-done(((bf16[1,2,12,640,160]{3,4,2,1,0:T(8,128)(2,1)}), bf16[4,2,12,640,160]{3,4,2,1,0:T(8,128)(2,1)}) %all-gather.2.cloned.1.call-update) | async-done | bytes 19660816 | tf_op jit(solution)/shard_map/all_gather | solution.py:74
  440.6 17.0 %copy.117 = bf16[4,2,12,640,160]{3,4,0,2,1:T(8,128)(2,1)} copy(bf16[4,2,12,640,160]{3,4,2,1,0:T(8,128)(2,1)} %all-gather.2.cloned.1.call-done) | data formatting | bytes 39321600 | tf_op jit(solution)/shard_map/all_gather | solution.py:74
  457.6 8.2 %fusion.46 = (bf16[1,12,640,4,160]{2,4,3,1,0:T(8,128)(2,1)S(1)}, bf16[1,12,640,4,160]{2,4,3,1,0:T(8,128)(2,1)S(1)}) fusion(bf16[2,12,640,4,160]{2,4,3,1,0:T(8,128)(2,1)} %bitcast.132), kind=kLoop, calls=%fused_computation.109 | loop fusion | bytes 39321600 | tf_op jit(solution)/shard_map/slice | solution.py:29
  465.8 0.0 copy-start.2
  465.8 2.5 fusion.48
  468.3 1.4 copy-done.2
  469.7 4.1 fusion.49
  473.8 6.5 subtract_bitcast_fusion.1
  480.3 4.9 add_bitcast_fusion.1
  485.2 5.1 fusion
  490.2 8.7 %fusion.5 = f32[12,640,160]{1,2,0:T(8,128)} fusion(bf16[12,640,640]{1,2,0:T(8,128)(2,1)} %bitcast.130, bf16[2,12,640,160]{2,3,1,0:T(8,128)(2,1)S(1)} %fusion), kind=kOutput, calls=%fused_computation.31 | convolution fusion | flops 1572864000 | bytes 17203200 | tf_op jit(solution)/shard_map/gjo,god->gjd/dot_general | solution.py:25
  499.0 2.5 fusion.6
  501.4 7.2 subtract_bitcast_fusion
  508.6 8.7 %add_bitcast_fusion = f32[1,12,640,160]{2,3,1,0:T(8,128)} fusion(f32[12,640,160]{1,2,0:T(8,128)S(1)} %fusion.6, bf16[12,640,640]{1,2,0:T(8,128)(2,1)} %bitcast.131, bf16[2,12,640,160]{2,3,1,0:T(8,128)(2,1)S(1)} %fusion), kind=kOutput, calls=%fused_computation.25 | convolution fusion | flops 1574092800 | bytes 22118400 | tf_op jit(solution)/shard_map/gjo,god->gjd/dot_general | solution.py:25
  517.3 7.4 fusion.4
  524.7 21.7 %subtract_convert_fusion.1 = bf16[1,12,640,160]{2,3,1,0:T(8,128)(2,1)S(1)} fusion(f32[2,12,640,160]{2,3,1,0:T(8,128)S(1)} %fusion.4, f32[12,160]{1,0:T(8,128)S(1)} %bitcast.137, f32[12,160]{1,0:T(8,128)S(1)} %bitcast.139, f32[12,160]{1,0:T(8,128)S(1)} %bitcast.141, f32[12,160]{1,0:T(8,128)S(1)} %bitcast.143, f32[12,160]{1,0:T(8,128)S(1)} %bitcast.145, ...), kind=kLoop, calls=%fused_computation.24 | loop fusion | flops 34406400 | bytes 22347776 | tf_op jit(solution)/shard_map/convert
  546.4 21.9 %add_convert_fusion = bf16[1,12,640,160]{2,3,1,0:T(8,128)(2,1)S(1)} fusion(f32[2,12,640,160]{2,3,1,0:T(8,128)S(1)} %fusion.4, f32[12,160]{1,0:T(8,128)S(1)} %bitcast.138, f32[12,160]{1,0:T(8,128)S(1)} %bitcast.140, f32[12,160]{1,0:T(8,128)S(1)} %bitcast.142, f32[12,160]{1,0:T(8,128)S(1)} %bitcast.144, f32[12,160]{1,0:T(8,128)S(1)} %bitcast.146, ...), kind=kLoop, calls=%fused_computation.23 | loop fusion | flops 34406400 | bytes 22347776 | tf_op jit(solution)/shard_map/convert.1
  568.3 2.7 pad_maximum_fusion
  571.0 19.4 %copy.74 = bf16[2,12,640,160]{3,0,1,2:T(2,128)(2,1)} copy(bf16[2,12,640,160]{2,3,1,0:T(8,128)(2,1)} %pad_maximum_fusion) | data formatting | bytes 9830400 | tf_op jit(solution)/shard_map/stack | solution.py:56
  590.5 177.8 %all_to_all.31 = bf16[2,12,640,160]{3,0,1,2:T(2,128)(2,1)S(1)} all-to-all(bf16[2,12,640,160]{3,0,1,2:T(2,128)(2,1)} %copy.74), channel_id=1, replica_groups=mesh['freq'=4,'panel'=8] {'panel'}, dimensions={2} | all-to-all | bytes 9830400 | tf_op jit(solution)/shard_map/all_to_all | solution.py:88
  768.2 4.9 copy.75
  773.1 0.0 copy-done.6
  773.1 27.9 %subtract_convert_fusion = bf16[80,160,1024]{2,1,0:T(8,128)(2,1)} fusion(bf16[80,160,1024]{2,1,0:T(8,128)(2,1)} %param.2, bf16[192,80,160]{2,1,0:T(8,128)(2,1)} %bitcast.136, f32[96,1024]{1,0:T(8,128)S(1)} %copy-done.6, f32[96,1024]{1,0:T(8,128)S(1)} %copy-done.4), kind=kOutput, calls=%fused_computation | convolution fusion | flops 5086380032 | bytes 58130432 | tf_op jit(solution)/shard_map/csr,ct->srt/dot_general | solution.py:92
  (26 shorter events, 0.1 us)
Async XLA Ops:
  6.5 252.1 %copy-start = (f32[16,7,64]{2,0,1:T(8,128)S(1)}, f32[16,7,64]{2,0,1:T(8,128)}, u32[]{:S(2)}) copy-start(f32[16,7,64]{2,0,1:T(8,128)} %param.3) | copy-start | bytes 86020
  6.5 434.0 %all-gather.2.cloned.1.call-start = ((), (), s32[]{:S(2)}) async-start(), calls=%async_computation.2 | async-start | bytes 24576000 | tf_op jit(solution)/shard_map/all_gather | solution.py:74
  8.2 0.7 copy-start.3
  8.2 0.9 copy-start.5
  465.8 3.9 copy-start.2
  768.2 4.9 copy-start.4
  768.2 4.9 copy-start.6
  773.1 27.9 %copy-start.1 = (f32[16,7,64]{2,0,1:T(8,128)S(1)}, f32[16,7,64]{2,0,1:T(8,128)}, u32[]{:S(2)}) copy-start(f32[16,7,64]{2,0,1:T(8,128)} %param.3) | copy-start | bytes 86020
Sparse Core Ops, SparseCore 0:
  258.7 181.7 all-gather.1
